TPU v7x, 32 devices: a whole 2x2x4 slice. The times are simulated.
32 devices in a mesh: row: 8 (over y, x, core), col: 4 (over z).
Axes of the slice: x: 2, y: 2, z: 4, core: 2. Of those that a mesh axis runs over, the one named last changes fastest.
Arguments:
- cam_jac: float32 [4, 2, 9, 4096], P(None, None, None, ('row', 'col')), may hold values from -0.6 to 0.6
- pt_jac: float32 [4, 2, 3, 4096], P(None, None, None, ('row', 'col')), may hold values from -6 to 6
- track_owner: int32 [4096, 4], P(('row', 'col')), may hold values from 0 to 31, all different within a row; in each aligned block of 128 rows (0 to 127, 128 to 255, ...) at most 32 rows name the same one
- track_cam: int32 [4096, 4], P(('row', 'col')), may hold values from 0 to 15
Outputs:
- reduced_system: float32 [4608, 4608], P(('row', 'col'))
Inputs may be any that keep to these rules, and one draw needn't show every extreme that they name: `track_owner`: the 4 observations of a point lie in 4 different blocks. Among the points of one device no block is named by more than 32 observations.
All inputs are finite; a program needn't handle non-finite values.
Results may differ from a plain program's by a relative error of at most 0.0001.
Values sent between devices are 32-bit elements; how exact they have to be, the bound alone decides.
A program may use at most 128 MiB of HBM per device.

v0:
```python
import jax
import jax.numpy as jnp
from jax import lax
from jax.sharding import PartitionSpec as P

CAM_TILE = 64


point_damping = 1.0


def eliminate(cam_jac, pt_jac):
    exact_precision = lax.Precision.HIGHEST
    normal = jnp.einsum("ktin,ktjn->ijn", pt_jac, pt_jac, precision=exact_precision)
    pivot_first = jnp.sqrt(normal[0, 0] + point_damping)
    below_first = normal[1, 0] / pivot_first
    below_second = normal[2, 0] / pivot_first
    pivot_second = jnp.sqrt(normal[1, 1] + point_damping - below_first * below_first)
    below_middle = (normal[2, 1] - below_second * below_first) / pivot_second
    pivot_third = jnp.sqrt(
        normal[2, 2] + point_damping - below_second * below_second - below_middle * below_middle
    )
    coupled = jnp.einsum("ktpn,ktrn->kprn", cam_jac, pt_jac, precision=exact_precision)
    column_first = coupled[:, :, 0] / pivot_first
    column_second = (coupled[:, :, 1] - column_first * below_first) / pivot_second
    third_column_block = (
        coupled[:, :, 2] - column_first * below_second - column_second * below_middle
    ) / pivot_third
    return jnp.stack([column_first, column_second, third_column_block], axis=2)


def shards(cam_jac, pt_jac, track_owner, track_cam):
    exact_precision = lax.Precision.HIGHEST
    obs_count = cam_jac.shape[0]
    point_count = cam_jac.shape[3]
    row_count = lax.axis_size("row")
    col_count = lax.axis_size("col")
    device_count = row_count * col_count
    cams_device = CAM_TILE // col_count
    camera_total = cams_device * device_count
    slot_count = 2 * point_count * obs_count // device_count
    width = obs_count * 27 + 18
    eliminated = eliminate(cam_jac, pt_jac)
    blocks = jnp.transpose(eliminated, (3, 0, 1, 2)).reshape(point_count, 1, obs_count * 27)
    blocks = jnp.broadcast_to(blocks, (point_count, obs_count, obs_count * 27))
    own_rows = jnp.transpose(cam_jac, (3, 0, 1, 2)).reshape(point_count, obs_count, 18)
    message_contents = jnp.concatenate([blocks, own_rows], axis=2).reshape(
        point_count * obs_count, width
    )
    camera = track_owner * cams_device + track_cam
    which_obs = jnp.broadcast_to(
        jnp.arange(obs_count, dtype=jnp.int32)[None, :, None], (point_count, obs_count, 1)
    )
    labels = jnp.concatenate(
        [jnp.broadcast_to(camera[:, None, :], (point_count, obs_count, obs_count)), which_obs],
        axis=2,
    )
    labels = labels.reshape(point_count * obs_count, obs_count + 1)
    target = track_owner.reshape(-1)
    onehot = (target[:, None] == jnp.arange(device_count, dtype=jnp.int32)[None, :]).astype(
        jnp.int32
    )
    before = jnp.cumsum(onehot, axis=0) - onehot
    slot_location = jnp.sum(before * onehot, axis=1)
    send_vals = (
        jnp.zeros((device_count, slot_count, width), jnp.float32)
        .at[target, slot_location]
        .set(message_contents)
    )
    filler_cams = jnp.broadcast_to(
        (jnp.arange(device_count, dtype=jnp.int32) * cams_device)[:, None, None],
        (device_count, slot_count, obs_count),
    )
    filler = jnp.concatenate(
        [filler_cams, jnp.zeros((device_count, slot_count, 1), jnp.int32)], axis=2
    )
    send_ints = filler.at[target, slot_location].set(labels)
    got_vals, got_ints = (
        lax.all_to_all(send_vals, ("row", "col"), split_axis=0, concat_axis=0, tiled=True),
        lax.all_to_all(send_ints, ("row", "col"), split_axis=0, concat_axis=0, tiled=True),
    )
    message_count = device_count * slot_count
    vals_last = jnp.transpose(got_vals.reshape(message_count, width))
    final_integer_grid = jnp.transpose(got_ints.reshape(message_count, obs_count + 1))
    anchor_index = final_integer_grid[obs_count]
    partners = final_integer_grid[:obs_count]
    picked = jnp.arange(obs_count, dtype=jnp.int32)[:, None] == anchor_index[None, :]
    chosen = picked.astype(jnp.float32)
    partner_blocks = vals_last[: obs_count * 27].reshape(obs_count, 9, 3, message_count)
    pinned_camera_rows = vals_last[obs_count * 27 :].reshape(2, 9, message_count)
    anchor_block = jnp.sum(chosen[:, None, None, :] * partner_blocks, axis=0)
    anchor_cam = jnp.sum(picked.astype(jnp.int32) * partners, axis=0)
    coupling = -jnp.einsum(
        "prm,kqrm->kpqm", anchor_block, partner_blocks, precision=exact_precision
    )
    self_coupling_term = jnp.einsum(
        "brd,bxd->rxd", pinned_camera_rows, pinned_camera_rows, precision=exact_precision
    )
    block_terms = coupling + chosen[:, None, None, :] * self_coupling_term[None]
    first_cam = lax.axis_index(("row", "col")) * cams_device
    segment = (anchor_cam - first_cam)[None, :] * camera_total + partners
    terms_rows = jnp.transpose(
        block_terms.reshape(obs_count, 81, message_count), (0, 2, 1)
    ).reshape(obs_count * message_count, 81)
    summed = jax.ops.segment_sum(
        terms_rows, segment.reshape(-1), num_segments=cams_device * camera_total
    )
    return jnp.transpose(summed.reshape(cams_device, camera_total, 9, 9), (0, 2, 1, 3)).reshape(
        cams_device * 9, camera_total * 9
    )


def solution(mesh):
    placed = (
        P(None, None, None, ("row", "col")),
        P(None, None, None, ("row", "col")),
        P(("row", "col"), None),
        P(("row", "col"), None),
    )
    return jax.shard_map(
        shards, mesh=mesh, in_specs=placed, out_specs=P(("row", "col"), None), check_vma=False
    )
```

profile of v0, /device:TPU:0, one launch (start us, length us, event | category | flops | bytes accessed | tf_op | source)
XLA Modules:
  0.0 304.0 jit_solution(16924132919376490271)
XLA Ops:
  0.0 0.8 copy.118
  0.8 0.1 eq.49
  0.9 0.1 eq.45
  1.0 0.1 reshape.126
  1.1 0.7 multiply_add_fusion
  1.8 1.2 reduce-window.6
  3.0 0.2 slice_reduce_fusion
  3.3 0.2 copy.148
  3.5 0.1 broadcast_in_dim.15
  3.6 0.1 fusion.4
  3.8 24.2 %scatter_fusion = s32[32,32,5]{2,1,0:T(8,128)S(1)} fusion(s32[32,32,5]{2,1,0:T(8,128)S(1)} %concatenate.18, s32[512]{0:T(512)S(1)} %bitcast.90, s32[512,5]{1,0:T(8,128)S(1)} %bitcast.100), kind=kCustom, calls=%fused_computation | custom fusion | bytes 34816 | tf_op jit(solution)/shard_map/scatter | solution.py:77
  28.0 0.3 copy.124
  28.3 0.7 reshape.164
  29.0 7.3 %all-to-all-start = ((s32[32,1,160]{2,1,0:T(1,128)}), s32[32,1,160]{2,1,0:T(1,128)S(1)}, u32[]{:S(2)}, u32[]{:S(2)}) async-start(s32[32,1,160]{2,1,0:T(1,128)} %reshape.164), calls=%async_computation | async-start | bytes 65536 | tf_op jit(solution)/shard_map/all_to_all | solution.py:80
  36.3 0.3 copy.130
  36.6 0.3 copy.126
  36.9 0.3 copy.127
  37.2 0.4 copy.134
  37.5 0.3 concatenate.22
  37.8 1.3 convolution_bitcast_fusion.1
  39.1 0.1 copy.131
  39.3 4.3 %fusion.17 = f32[4,128,3,9]{3,2,1,0:T(4,128)S(1)} fusion(f32[4,2,3,128]{2,1,3,0:T(2,128)S(1)} %copy.126, f32[4,2,9,128]{2,1,3,0:T(2,128)S(1)} %copy.127), kind=kOutput, calls=%fused_computation.55 | convolution fusion | flops 331776 | bytes 104448 | tf_op jit(solution)/shard_map/ktpn,ktrn->kprn/dot_general | solution.py:23
  43.5 0.3 copy.128
  44.1 0.1 pad_maximum_fusion
  44.3 0.9 broadcast_in_dim.18
  45.1 54.5 %scatter_fusion.1 = f32[32,32,126]{2,1,0:T(8,128)} fusion(f32[32,32,126]{2,1,0:T(8,128)} %broadcast_in_dim.18, s32[512]{0:T(512)S(1)} %bitcast.91, f32[512,126]{1,0:T(8,128)S(1)} %pad_maximum_fusion), kind=kCustom, calls=%fused_computation.1 | custom fusion | bytes 778240 | tf_op jit(solution)/shard_map/scatter | solution.py:68
  99.6 6.0 %all-to-all-start.1 = ((f32[32,32,126]{2,1,0:T(8,128)}), f32[32,32,126]{2,1,0:T(8,128)S(1)}, u32[]{:S(2)}, u32[]{:S(2)}) async-start(f32[32,32,126]{2,1,0:T(8,128)} %scatter_fusion.1), calls=%async_computation.1 | async-start | bytes 1048576 | tf_op jit(solution)/shard_map/all_to_all | solution.py:79
  105.6 0.6 broadcast.171
  106.2 0.8 reduce.2
  107.3 1.1 copy.138
  108.4 11.3 %all-to-all-done.1 = f32[32,32,126]{2,1,0:T(8,128)S(1)} async-done(((f32[32,32,126]{2,1,0:T(8,128)}), f32[32,32,126]{2,1,0:T(8,128)S(1)}, u32[]{:S(2)}, u32[]{:S(2)}) %all-to-all-start.1) | async-done | bytes 516128 | tf_op jit(solution)/shard_map/all_to_all | solution.py:79
  119.7 0.2 slice.77
  119.9 0.2 copy.135
  120.1 0.2 reshape.131
  120.3 0.2 multiply_reduce_fusion
  120.5 6.2 %copy.136 = f32[4,9,3,1024]{1,2,0,3:T(4,128)} copy(f32[4,9,3,1024]{3,2,1,0:T(4,128)S(1)} %reshape.131) | data formatting | bytes 884736 | tf_op jit(solution)/shard_map/reshape | solution.py:89
  126.7 0.6 reshape.160
  127.3 0.9 copy.147
  128.2 13.5 %convolution_bitcast_fusion = f32[9,9,1024]{0,1,2:T(8,128)S(1)} fusion(f32[2,9,1024]{1,0,2:T(2,128)S(1)} %reshape.160), kind=kOutput, calls=%fused_computation.4 | convolution fusion | flops 1990656 | bytes 405504 | tf_op jit(solution)/shard_map/brd,bxd->rxd/dot_general | solution.py:96
  141.7 63.0 %bitcast_add_fusion = f32[4,9,9,1024]{1,2,0,3:T(8,128)} fusion(f32[9,9,1024]{0,1,2:T(8,128)S(1)} %convolution_bitcast_fusion, f32[4,1024]{0,1:T(8,128)S(1)} %copy-done.1, f32[4,9,3,1024]{1,2,0,3:T(4,128)S(1)} %copy-done, f32[9,3,1024,1]{0,1,3,2:T(4,128)S(1)} %copy.147), kind=kOutput, calls=%fused_computation.3 | convolution fusion | flops 12939264 | bytes 2228224 | tf_op jit(solution)/shard_map/prm,kqrm->kpqm/dot_general | solution.py:93
  204.8 23.3 %copy.142 = f32[4,9,9,1024]{3,0,2,1:T(4,128)S(1)} copy(f32[4,9,9,1024]{1,2,0,3:T(8,128)} %bitcast_add_fusion) | data formatting | bytes 2654208 | tf_op jit(solution)/shard_map/add | solution.py:99
  228.1 0.8 copy.151
  229.0 24.5 %scatter_custom_fusion.2 = f32[8192,81]{1,0:T(8,128)} fusion(s32[4096]{0:T(1024)S(1)} %bitcast.111, f32[4096,81]{1,0:T(8,128)S(1)} %bitcast.98, f32[]{:T(128)} %constant.10.clone.1), kind=kCustom, calls=%fused_computation.5 | custom fusion | flops 331776 | bytes 2654212 | tf_op jit(solution)/shard_map/scatter-add | solution.py:105
  253.5 3.8 %copy.144 = f32[8192,81]{0,1:T(8,128)S(1)} copy(f32[8192,81]{1,0:T(8,128)} %scatter_custom_fusion.2) | data formatting | bytes 5308416 | tf_op jit(solution)/shard_map/scatter-add | solution.py:105
  257.3 1.9 copy.155
  259.2 0.2 slice.78
  259.5 19.4 %copy.145 = f32[16,9,512,9]{3,2,1,0:T(8,128)} copy(f32[16,9,512,9]{2,0,3,1:T(8,128)S(1)} %bitcast.94) | data formatting | bytes 5308416 | tf_op jit(solution)/shard_map/transpose | solution.py:108
  278.8 25.2 %reshape.136 = f32[144,4608]{1,0:T(8,128)} reshape(f32[16,9,512,9]{3,2,1,0:T(8,128)} %copy.145) | data formatting | bytes 5308416 | tf_op jit(solution)/shard_map/reshape | solution.py:108
  (34 shorter events, 0.7 us)
Async XLA Ops:
  0.0 36.3 %copy-start.3 = (f32[4,2,3,128]{3,1,2,0:T(2,128)S(1)}, f32[4,2,3,128]{3,1,2,0:T(2,128)}, u32[]{:S(2)}) copy-start(f32[4,2,3,128]{3,1,2,0:T(2,128)} %param.5) | copy-start | bytes 36868
  3.5 33.4 %copy-start.2 = (f32[4,2,9,128]{3,1,2,0:T(2,128)S(1)}, f32[4,2,9,128]{3,1,2,0:T(2,128)}, u32[]{:S(2)}) copy-start(f32[4,2,9,128]{3,1,2,0:T(2,128)} %param.4) | copy-start | bytes 110596
  29.0 70.6 %all-to-all-start = ((s32[32,1,160]{2,1,0:T(1,128)}), s32[32,1,160]{2,1,0:T(1,128)S(1)}, u32[]{:S(2)}, u32[]{:S(2)}) async-start(s32[32,1,160]{2,1,0:T(1,128)} %reshape.164), calls=%async_computation | async-start | bytes 65536 | tf_op jit(solution)/shard_map/all_to_all | solution.py:80
  99.6 20.0 %all-to-all-start.1 = ((f32[32,32,126]{2,1,0:T(8,128)}), f32[32,32,126]{2,1,0:T(8,128)S(1)}, u32[]{:S(2)}, u32[]{:S(2)}) async-start(f32[32,32,126]{2,1,0:T(8,128)} %scatter_fusion.1), calls=%async_computation.1 | async-start | bytes 1048576 | tf_op jit(solution)/shard_map/all_to_all | solution.py:79
  128.2 13.5 %copy-start = (f32[4,9,3,1024]{1,2,0,3:T(4,128)S(1)}, f32[4,9,3,1024]{1,2,0,3:T(4,128)}, u32[]{:S(2)}) copy-start(f32[4,9,3,1024]{1,2,0,3:T(4,128)} %copy.136) | copy-start | bytes 1327108
  128.2 13.5 %copy-start.1 = (f32[4,1024]{0,1:T(8,128)S(1)}, f32[4,1024]{0,1:T(8,128)}, u32[]{:S(2)}) copy-start(f32[4,1024]{0,1:T(8,128)} %copy.138) | copy-start | bytes 49156
where the time goes:
time: 308 us; the launch traced here: 304 us
  local copies, waits for them, and re-layouts  169 us (55%)
  matrix products  82.1 us (27%)
  other arithmetic  27.7 us (9%)
  starting transfers between devices  13.2 us (4%)
  waiting for transfers between devices  11.3 us (4%)
    dot_general x1, matrix products, shards(): jnp.einsum('prm,kqrm->kpqm', anchor_block, partner_blocks, precision=exac...  63 us
    scatter x1, local copies, waits for them, and re-layouts, shards(): send_vals = jnp.zeros((device_count, slot_count, width), jnp.float32).at[...  54.5 us
    reshape x1, local copies, waits for them, and re-layouts, shards(): jnp.transpose(summed.reshape(cams_device, camera_total, 9, 9), (0, 2, 1, 3))  25.2 us
    scatter x2, local copies, waits for them, and re-layouts, shards(): send_ints = filler.at[target, slot_location].set(labels)  24.5 us
    scatter-add x1, other arithmetic, shards(): jax.ops.segment_sum(terms_rows, segment.reshape(-1), num_segments=cams_de...  24.5 us
    add x1, local copies, waits for them, and re-layouts, shards(): block_terms = coupling + chosen[:, None, None, :] * self_coupling_term[None]  23.3 us
    transpose x1, local copies, waits for them, and re-layouts, shards(): jnp.transpose(summed.reshape(cams_device, camera_total, 9, 9), (0, 2, 1, 3))  19.4 us
    dot_general x1, matrix products, shards(): jnp.einsum('brd,bxd->rxd', pinned_camera_rows, pinned_camera_rows, precis...  13.5 us
  transfers between devices with their start and end apart: 2, of which 1 were waited for; matrix products, arithmetic and copies ran while one was open for 22% of the time, Pallas kernels for 0%

commit v1 on v0

v1 whole, which is shorter than its diff:
```python
import functools
import jax
import jax.numpy as jnp
from jax import lax
from jax.experimental import pallas as pl
from jax.experimental.pallas import tpu as pltpu
from jax.sharding import PartitionSpec as P

CAM_TILE = 64
GROUP = 128
point_damping = 1.0
NT = (((1,), (1,)), ((), ()))
NN = (((1,), (0,)), ((), ()))


def split(x):
    high = x.astype(jnp.bfloat16)
    return high, (x - high.astype(jnp.float32)).astype(jnp.bfloat16)


def dot(a, b, dims):
    return lax.dot_general(a, b, dims, preferred_element_type=jnp.float32)


def assemble(obs, cams_device, me_ref, got_ref, out_ref,
             lhs_ref, elim_ref, rhs_ref, perm_ref, ids_ref, own_ref):
    step = pl.program_id(0)
    total = got_ref.shape[0]
    rows = cams_device * 9
    owners = GROUP // cams_device
    me = me_ref[0]
    first = me * cams_device

    @pl.when(step == 0)
    def _():
        feats = jnp.transpose(got_ref[...])
        cam = [[feats[(k * 2 + t) * 9:(k * 2 + t) * 9 + 9] for t in range(2)] for k in range(obs)]
        base = obs * 18
        pt = [[[feats[base + (k * 2 + t) * 3 + r:base + (k * 2 + t) * 3 + r + 1]
                for r in range(3)] for t in range(2)] for k in range(obs)]
        ids = feats[base + obs * 6:base + obs * 7].astype(jnp.int32)
        ids_ref[:obs] = ids

        def normal(i, j):
            return sum(pt[k][t][i] * pt[k][t][j] for k in range(obs) for t in range(2))

        pivot_first = jnp.sqrt(normal(0, 0) + point_damping)
        below_first = normal(1, 0) / pivot_first
        below_second = normal(2, 0) / pivot_first
        pivot_second = jnp.sqrt(normal(1, 1) + point_damping - below_first * below_first)
        below_middle = (normal(2, 1) - below_second * below_first) / pivot_second
        pivot_third = jnp.sqrt(normal(2, 2) + point_damping - below_second * below_second
                               - below_middle * below_middle)
        elim = []
        for k in range(obs):
            coupled = [cam[k][0] * pt[k][0][r] + cam[k][1] * pt[k][1][r] for r in range(3)]
            one = coupled[0] / pivot_first
            two = (coupled[1] - one * below_first) / pivot_second
            three = (coupled[2] - one * below_second - two * below_middle) / pivot_third
            elim.append([one, two, three])
            high, low = split(jnp.concatenate([one, two, three], axis=0))
            elim_ref[0, k] = high.astype(jnp.float32)
            elim_ref[1, k] = low.astype(jnp.float32)

        mine = [(ids[k:k + 1] >= first) & (ids[k:k + 1] < first + cams_device) for k in range(obs)]
        place = jnp.zeros((1, total), jnp.int32)
        for k in range(obs):
            place = jnp.where(mine[k], ids[k:k + 1] - first, place)
        owner_row = lax.broadcasted_iota(jnp.int32, (rows, total), 0) // 9
        spread = (lax.broadcasted_iota(jnp.int32, (rows, 16), 0) % 9
                  == lax.broadcasted_iota(jnp.int32, (rows, 16), 1)).astype(jnp.bfloat16)
        keep = owner_row == place

        def tiled(piece):
            pad = jnp.concatenate([piece, jnp.zeros((7, total), jnp.float32)], axis=0)
            high, low = split(pad)
            return [jnp.where(keep, dot(spread, part, NN), 0.0).astype(jnp.bfloat16)
                    for part in (high, low)]

        for r in range(3):
            anchor = sum(jnp.where(mine[k], elim[k][r], 0.0) for k in range(obs))
            high, low = tiled(-anchor)
            lhs_ref[:rows, r * total:(r + 1) * total] = high
            lhs_ref[rows:, r * total:(r + 1) * total] = low

        diag = jnp.zeros((rows, rows), jnp.float32)
        for t in range(2):
            anchor = sum(jnp.where(mine[k], cam[k][t], 0.0) for k in range(obs))
            high, low = tiled(anchor)
            both = dot(jnp.concatenate([high, low], axis=0), high, NT)
            diag = diag + both[:rows] + both[rows:] + dot(high, low, NT)
        same = (lax.broadcasted_iota(jnp.int32, (rows, rows), 0) // 9
                == lax.broadcasted_iota(jnp.int32, (rows, rows), 1) // 9)
        own_ref[...] = jnp.where(same, diag, 0.0)

        source = lax.broadcasted_iota(jnp.int32, (9 * GROUP, 1), 0)
        goal = (source % GROUP) * 9 + source // GROUP
        perm_ref[...] = (lax.broadcasted_iota(jnp.int32, (9 * GROUP, 9 * GROUP), 1) == goal
                         ).astype(jnp.bfloat16)

    cam_row = lax.broadcasted_iota(jnp.int32, (cams_device, total), 0)

    for j in range(owners):
        start = step * GROUP + j * cams_device
        ids = ids_ref[:obs]
        named = [(ids[k:k + 1] >= start) & (ids[k:k + 1] < start + cams_device) for k in range(obs)]
        place = jnp.full((1, total), -1, jnp.int32)
        for k in range(obs):
            place = jnp.where(named[k], ids[k:k + 1] - start, place)
        mask = cam_row == place
        for part in range(2):
            chosen = jnp.zeros((27, total), jnp.float32)
            for k in range(obs):
                chosen = jnp.where(named[k], elim_ref[part, k], chosen)
            for r in range(3):
                for q in range(9):
                    at = q * GROUP + j * cams_device
                    rhs_ref[part, at:at + cams_device, r * total:(r + 1) * total] = jnp.where(
                        mask, chosen[r * 9 + q:r * 9 + q + 1], 0.0).astype(jnp.bfloat16)

    both = dot(lhs_ref[...], rhs_ref[0], NT)
    block = both[:rows] + both[rows:] + dot(lhs_ref[:rows], rhs_ref[1], NT)
    high, low = split(block)
    both = dot(jnp.concatenate([high, low], axis=0), perm_ref[...], NN)
    out_ref[...] = both[:rows] + both[rows:]

    @pl.when(me // owners == step)
    def _():
        put = (lax.broadcasted_iota(jnp.int32, (rows, 9 * GROUP), 1)
               == lax.broadcasted_iota(jnp.int32, (rows, 9 * GROUP), 0)
               + (me % owners) * rows).astype(jnp.bfloat16)
        high, low = split(own_ref[...])
        out_ref[...] += dot(high, put, NN) + dot(low, put, NN)


def shards(cam_jac, pt_jac, track_owner, track_cam):
    obs = cam_jac.shape[0]
    points = cam_jac.shape[3]
    device_count = lax.axis_size("row") * lax.axis_size("col")
    cams_device = CAM_TILE // lax.axis_size("col")
    slots = 2 * points * obs // device_count
    rows = cams_device * 9
    total = device_count * slots

    camera = track_owner * cams_device + track_cam
    data = jnp.concatenate([
        cam_jac.reshape(obs * 18, points),
        pt_jac.reshape(obs * 6, points),
        jnp.transpose(camera).astype(jnp.float32),
        jnp.zeros((128 - obs * 25, points), jnp.float32),
    ], axis=0)
    devices = jnp.arange(device_count, dtype=jnp.int32)
    names = jnp.any(track_owner[:, :, None] == devices, axis=1)
    earlier = jnp.tril(jnp.ones((points, points), jnp.bfloat16), -1)
    rank = jnp.einsum("mn,nd->dm", earlier, names.astype(jnp.bfloat16),
                      preferred_element_type=jnp.float32)
    pick = jnp.where(
        names.T[:, None, :]
        & (rank[:, None, :] == jnp.arange(slots, dtype=jnp.float32)[None, :, None]), 1.0, 0.0)
    send = lax.dot_general(pick.reshape(total, points), data, NT,
                           precision=lax.Precision.HIGHEST,
                           preferred_element_type=jnp.float32)
    got = lax.all_to_all(send.reshape(device_count, slots, 128), ("row", "col"),
                         split_axis=0, concat_axis=0, tiled=True).reshape(total, 128)
    me = lax.axis_index(("row", "col")).astype(jnp.int32).reshape(1)
    steps = device_count * cams_device // GROUP
    return pl.pallas_call(
        functools.partial(assemble, obs, cams_device),
        grid=(steps,),
        out_shape=jax.ShapeDtypeStruct((rows, device_count * rows), jnp.float32),
        in_specs=[pl.BlockSpec(memory_space=pltpu.SMEM),
                  pl.BlockSpec((total, 128), lambda i: (0, 0))],
        out_specs=pl.BlockSpec((rows, 9 * GROUP), lambda i: (0, i)),
        scratch_shapes=[
            pltpu.VMEM((2 * rows, 3 * total), jnp.bfloat16),
            pltpu.VMEM((2, obs, 27, total), jnp.float32),
            pltpu.VMEM((2, 9 * GROUP, 3 * total), jnp.bfloat16),
            pltpu.VMEM((9 * GROUP, 9 * GROUP), jnp.bfloat16),
            pltpu.VMEM((8, total), jnp.int32),
            pltpu.VMEM((rows, rows), jnp.float32),
        ],
        compiler_params=pltpu.CompilerParams(
            dimension_semantics=("arbitrary",), vmem_limit_bytes=60 * 1024 * 1024),
    )(me, got)


def solution(mesh):
    placed = (
        P(None, None, None, ("row", "col")),
        P(None, None, None, ("row", "col")),
        P(("row", "col"), None),
        P(("row", "col"), None),
    )
    return jax.shard_map(
        shards, mesh=mesh, in_specs=placed, out_specs=P(("row", "col"), None), check_vma=False
    )
```

time: 308 us -> 60.8 us (0.20)
  local copies, waits for them, and re-layouts: 169 us -> 2.37 us
  matrix products: 82.1 us -> 1.68 us
  Pallas kernels: 0 us -> 32.5 us
  other arithmetic: 27.7 us -> 1.4 us
  starting transfers between devices: 13.2 us -> 7.32 us
    dot_general x4 -> x2, matrix products: 82.1 us -> 1.68 us  [the longest x1 1.49 us: shards(): lax.dot_general(pick.reshape(total, points), data, NT, precision=lax.Prec...]
    scatter x3 -> x0, local copies, waits for them, and re-layouts: 79 us -> none  [the longest x1 54.5 us: shards(): send_vals = jnp.zeros((device_count, slot_count, width), jnp.float32).at[...]
    reshape x8 -> x2, local copies, waits for them, and re-layouts: 33.5 us -> 0.02 us  [the longest x1 0.01 us: shards(): pt_jac.reshape(obs * 6, points)]
    pallas_call x0 -> x1, Pallas kernels: none -> 32.5 us  [shards(): pl.pallas_call(functools.partial(assemble, obs, cams_device), grid=(steps...]
    scatter-add x1 -> x0, other arithmetic: 24.5 us -> none  [shards(): jax.ops.segment_sum(terms_rows, segment.reshape(-1), num_segments=cams_de...]
    add x1 -> x0, local copies, waits for them, and re-layouts: 23.3 us -> none  [shards(): block_terms = coupling + chosen[:, None, None, :] * self_coupling_term[None]]
    transpose x3 -> x0, local copies, waits for them, and re-layouts: 19.7 us -> none  [the longest x1 19.4 us: shards(): jnp.transpose(summed.reshape(cams_device, camera_total, 9, 9), (0, 2, 1, 3))]
    all_to_all x2 -> x1, starting transfers between devices: 13.2 us -> 7.32 us  [shards(): lax.all_to_all(send.reshape(device_count, slots, 128), ('row', 'col'), sp...]
  transfers between devices with their start and end apart: 2 -> 1, of which waited for: 1 -> 1; matrix products, arithmetic and copies ran while one was open for 22% -> 0% of each run, Pallas kernels for 0% -> 0%
where the time goes in v1:
time: 60.8 us; the launch traced here: 59.6 us
  Pallas kernels  32.5 us (53%)
  waiting for transfers between devices  14.2 us (23%)
  starting transfers between devices  7.32 us (12%)
  local copies, waits for them, and re-layouts  2.37 us (4%)
  matrix products  1.68 us (3%)
  other arithmetic  1.4 us (2%)
    pallas_call x1, Pallas kernels, shards(): pl.pallas_call(functools.partial(assemble, obs, cams_device), grid=(steps...  32.5 us
    all_to_all x1, waiting for transfers between devices, shards(): lax.all_to_all(send.reshape(device_count, slots, 128), ('row', 'col'), sp...  14.2 us
    all_to_all x1, starting transfers between devices, shards(): lax.all_to_all(send.reshape(device_count, slots, 128), ('row', 'col'), sp...  7.32 us
    unnamed x4, local copies, waits for them, and re-layouts  2.27 us
    dot_general x1, matrix products, shards(): lax.dot_general(pick.reshape(total, points), data, NT, precision=lax.Prec...  1.49 us
  transfers between devices with their start and end apart: 1, of which 1 were waited for; matrix products, arithmetic and copies ran while one was open for 0% of the time, Pallas kernels for 0%

profile of v1, /device:TPU:0, one launch (start us, length us, event | category | flops | bytes accessed | tf_op | source)
XLA Modules:
  0.0 59.6 jit_solution(11920838019322100985)
XLA Ops:
  0.0 0.7 %fusion.13 = pred[128,32]{0,1:T(8,128)(4,1)S(1)} fusion(s32[128,4]{0,1:T(4,128)} %param.6), kind=kLoop, calls=%fused_computation.16 | loop fusion | flops 28672 | bytes 6144 | tf_op jit(solution)/shard_map/reduce_or | solution.py:153
  0.7 0.7 %convert_bitcast_fusion = f32[4,128]{1,0:T(4,128)S(1)} fusion(s32[128,4]{0,1:T(4,128)} %param.7, s32[128,4]{0,1:T(4,128)} %param.6), kind=kLoop, calls=%fused_computation.23 | loop fusion | flops 1536 | bytes 6144 | tf_op jit(solution)/shard_map/convert_element_type | solution.py:149
  1.4 0.7 %copy.12 = f32[4,2,3,128]{3,2,1,0:T(4,128)S(1)} copy(f32[4,2,3,128]{3,1,2,0:T(2,128)} %param.5) | data formatting | bytes 24576 | tf_op args[1]
  2.1 0.8 %copy.11 = f32[4,2,9,128]{3,2,1,0:T(8,128)S(1)} copy(f32[4,2,9,128]{3,1,2,0:T(2,128)} %param.4) | data formatting | bytes 73728 | tf_op args[0]
  2.9 0.1 pad.3.clone
  3.0 0.2 fusion.15
  3.2 1.5 %fusion = f32[32,32,128]{2,1,0:T(8,128)} fusion(f32[32,128]{1,0:T(8,128)S(1)} %fusion.15, pred[32,128]{1,0:T(8,128)(4,1)S(1)} %bitcast.10, f32[4,128]{1,0:T(4,128)S(1)} %convert_bitcast_fusion, f32[24,128]{1,0:T(8,128)S(1)} %reshape.28, f32[72,128]{1,0:T(8,128)S(1)} %reshape.27, f32[128]{0:T(128)S(1)} %pad.3.clone), kind=kOutput, calls=%fused_computation | convolution fusion | flops 201768960 | bytes 596480 | tf_op jit(solution)/shard_map/dot_general | solution.py:160
  4.7 7.3 %all-to-all-start = ((f32[32,32,128]{2,1,0:T(8,128)}), f32[32,32,128]{2,1,0:T(8,128)S(1)}, u32[]{:S(2)}, u32[]{:S(2)}) async-start(f32[32,32,128]{2,1,0:T(8,128)} %fusion), calls=%async_computation | async-start | bytes 1048576 | tf_op jit(solution)/shard_map/all_to_all | solution.py:163
  12.0 14.2 %all-to-all-done = f32[32,32,128]{2,1,0:T(8,128)S(1)} async-done(((f32[32,32,128]{2,1,0:T(8,128)}), f32[32,32,128]{2,1,0:T(8,128)S(1)}, u32[]{:S(2)}, u32[]{:S(2)}) %all-to-all-start) | async-done | bytes 524320 | tf_op jit(solution)/shard_map/all_to_all | solution.py:163
  26.3 0.0 copy-start
  26.3 0.8 %copy-done = f32[32,32,128]{2,1,0:T(8,128)} copy-done((f32[32,32,128]{2,1,0:T(8,128)}, f32[32,32,128]{2,1,0:T(8,128)S(1)}, u32[]{:S(2)}) %copy-start) | copy-done | bytes 524312
  27.0 32.5 %shard_map.46 = f32[144,4608]{1,0:T(8,128)} custom-call(s32[1]{0:T(128)} %bitcast.me_ref, f32[1024,128]{1,0:T(8,128)} %bitcast.9), custom_call_target="tpu_custom_call" | custom-call | tf_op jit(solution)/shard_map/pallas_call | solution.py:167
  (4 shorter events, 0.0 us)
Async XLA Ops:
  4.7 21.6 %all-to-all-start = ((f32[32,32,128]{2,1,0:T(8,128)}), f32[32,32,128]{2,1,0:T(8,128)S(1)}, u32[]{:S(2)}, u32[]{:S(2)}) async-start(f32[32,32,128]{2,1,0:T(8,128)} %fusion), calls=%async_computation | async-start | bytes 1048576 | tf_op jit(solution)/shard_map/all_to_all | solution.py:163
  26.3 0.8 %copy-start = (f32[32,32,128]{2,1,0:T(8,128)}, f32[32,32,128]{2,1,0:T(8,128)S(1)}, u32[]{:S(2)}) copy-start(f32[32,32,128]{2,1,0:T(8,128)S(1)} %all-to-all-done) | copy-start | bytes 1572868

commit v2 on v1

--- a/solution.py
+++ b/solution.py
@@ -131,6 +131,38 @@
                + (me % owners) * rows).astype(jnp.bfloat16)
         high, low = split(own_ref[...])
         out_ref[...] += dot(high, put, NN) + dot(low, put, NN)
+
+
+def exchange(count, cols, send_ref, out_ref, got_ref, send_sem, recv_sem):
+    me = lax.axis_index("row") * cols + lax.axis_index("col")
+    barrier = pltpu.get_barrier_semaphore()
+
+    def spot(shift):
+        peer = lax.rem(me + shift, count)
+        return peer, (lax.div(peer, cols), lax.rem(peer, cols))
+
+    for shift in range(1, count):
+        pl.semaphore_signal(barrier, inc=1, device_id=spot(shift)[1],
+                            device_id_type=pl.DeviceIdType.MESH)
+    pl.semaphore_wait(barrier, count - 1)
+    copies = []
+    for shift in range(1, count):
+        peer, where = spot(shift)
+        copy = pltpu.make_async_remote_copy(
+            src_ref=send_ref.at[peer],
+            dst_ref=got_ref.at[shift],
+            send_sem=send_sem.at[shift],
+            recv_sem=recv_sem.at[shift],
+            device_id=where,
+            device_id_type=pl.DeviceIdType.MESH,
+        )
+        copy.start()
+        copies.append(copy)
+    out_ref[0] = send_ref[me]
+    for copy in copies:
+        copy.wait()
+    for shift in range(1, count):
+        out_ref[shift] = got_ref[shift]
 
 
 def shards(cam_jac, pt_jac, track_owner, track_cam):
@@ -160,8 +192,19 @@
     send = lax.dot_general(pick.reshape(total, points), data, NT,
                            precision=lax.Precision.HIGHEST,
                            preferred_element_type=jnp.float32)
-    got = lax.all_to_all(send.reshape(device_count, slots, 128), ("row", "col"),
-                         split_axis=0, concat_axis=0, tiled=True).reshape(total, 128)
+    block = (device_count, slots, 128)
+    got = pl.pallas_call(
+        functools.partial(exchange, device_count, lax.axis_size("col")),
+        out_shape=jax.ShapeDtypeStruct(block, jnp.float32),
+        in_specs=[pl.BlockSpec(memory_space=pltpu.VMEM)],
+        out_specs=pl.BlockSpec(memory_space=pltpu.VMEM),
+        scratch_shapes=[
+            pltpu.VMEM(block, jnp.float32),
+            pltpu.SemaphoreType.DMA((device_count,)),
+            pltpu.SemaphoreType.DMA((device_count,)),
+        ],
+        compiler_params=pltpu.CompilerParams(collective_id=0, has_side_effects=True),
+    )(send.reshape(block)).reshape(total, 128)
     me = lax.axis_index(("row", "col")).astype(jnp.int32).reshape(1)
     steps = device_count * cams_device // GROUP
     return pl.pallas_call(

time: 60.8 us -> 59.6 us (0.980); the launches traced: 59.6 us -> 59.3 us
  Pallas kernels: 32.5 us -> 54.6 us
  waiting for transfers between devices: 14.2 us -> 0 us
  starting transfers between devices: 7.32 us -> 0 us
  local copies, waits for them, and re-layouts: 2.37 us -> 1.61 us
    pallas_call x0 -> x1, Pallas kernels: none -> 22 us  [shards(): pl.pallas_call(functools.partial(exchange, device_count, lax.axis_size('c...]
    all_to_all x1 -> x0, waiting for transfers between devices: 14.2 us -> none  [shards(): lax.all_to_all(send.reshape(device_count, slots, 128), ('row', 'col'), sp...]
    all_to_all x1 -> x0, starting transfers between devices: 7.32 us -> none  [shards(): lax.all_to_all(send.reshape(device_count, slots, 128), ('row', 'col'), sp...]
    unnamed x4 -> x2, local copies, waits for them, and re-layouts: 2.27 us -> 1.51 us
  transfers between devices with their start and end apart: 1 -> 0, of which waited for: 1 -> 0; matrix products, arithmetic and copies ran while one was open for 0% -> 0% of each run, Pallas kernels for 0% -> 0%
where the time goes in v2:
time: 59.6 us; the launch traced here: 59.3 us
  Pallas kernels  54.6 us (92%)
  matrix products  1.66 us (3%)
  local copies, waits for them, and re-layouts  1.61 us (3%)
  other arithmetic  1.4 us (2%)
    pallas_call x1, Pallas kernels, shards(): pl.pallas_call(functools.partial(assemble, obs, cams_device), grid=(steps...  32.6 us
    pallas_call x1, Pallas kernels, shards(): pl.pallas_call(functools.partial(exchange, device_count, lax.axis_size('c...  22 us
    unnamed x2, local copies, waits for them, and re-layouts  1.51 us
    dot_general x1, matrix products, shards(): lax.dot_general(pick.reshape(total, points), data, NT, precision=lax.Prec...  1.47 us

profile of v2, /device:TPU:0, one launch (start us, length us, event | category | flops | bytes accessed | tf_op | source)
XLA Modules:
  0.0 59.3 jit_solution(3555290029673964554)
XLA Ops:
  0.0 0.1 pad.3.clone
  0.1 0.7 %convert_bitcast_fusion = f32[4,128]{1,0:T(4,128)S(1)} fusion(s32[128,4]{0,1:T(4,128)} %param.7, s32[128,4]{0,1:T(4,128)} %param.6), kind=kLoop, calls=%fused_computation.23 | loop fusion | flops 1536 | bytes 6144 | tf_op jit(solution)/shard_map/convert_element_type | solution.py:181
  0.8 0.7 %fusion.13 = pred[128,32]{0,1:T(8,128)(4,1)S(1)} fusion(s32[128,4]{0,1:T(4,128)} %param.6), kind=kLoop, calls=%fused_computation.16 | loop fusion | flops 28672 | bytes 6144 | tf_op jit(solution)/shard_map/reduce_or | solution.py:185
  1.5 0.2 fusion.15
  1.7 0.7 %copy.12 = f32[4,2,3,128]{3,2,1,0:T(4,128)S(1)} copy(f32[4,2,3,128]{3,1,2,0:T(2,128)} %param.5) | data formatting | bytes 24576 | tf_op args[1]
  2.4 0.8 %copy.11 = f32[4,2,9,128]{3,2,1,0:T(8,128)S(1)} copy(f32[4,2,9,128]{3,1,2,0:T(2,128)} %param.4) | data formatting | bytes 73728 | tf_op args[0]
  3.2 1.5 %fusion.send_ref = f32[32,32,128]{2,1,0:T(8,128)} fusion(f32[32,128]{1,0:T(8,128)S(1)} %fusion.15, pred[32,128]{1,0:T(8,128)(4,1)S(1)} %bitcast.10, f32[4,128]{1,0:T(4,128)S(1)} %convert_bitcast_fusion, f32[24,128]{1,0:T(8,128)S(1)} %reshape.28, f32[72,128]{1,0:T(8,128)S(1)} %reshape.27, f32[128]{0:T(128)S(1)} %pad.3.clone), kind=kOutput, calls=%fused_computation | convolution fusion | flops 201768960 | bytes 596480 | tf_op jit(solution)/shard_map/dot_general | solution.py:192
  4.7 22.0 %shard_map.46 = f32[32,32,128]{2,1,0:T(8,128)} custom-call(f32[32,32,128]{2,1,0:T(8,128)} %fusion.send_ref), custom_call_target="tpu_custom_call" | custom-call | tf_op jit(solution)/shard_map/pallas_call | solution.py:196
  26.7 32.6 %shard_map.47 = f32[144,4608]{1,0:T(8,128)} custom-call(s32[1]{0:T(128)} %bitcast.me_ref, f32[1024,128]{1,0:T(8,128)} %bitcast.9), custom_call_target="tpu_custom_call" | custom-call | tf_op jit(solution)/shard_map/pallas_call | solution.py:210
  (4 shorter events, 0.0 us)
